TPU v7x, 32 devices: a whole 2x2x4 slice. The times are simulated.
32 devices in a mesh: tm: 8 (over y, x, core), chan: 4 (over z).
Axes of the slice: x: 2, y: 2, z: 4, core: 2. Of those that a mesh axis runs over, the one named last changes fastest.
Arguments:
- volts: bfloat16 [4, 16, 12288, 256], P(None, 'chan', 'tm'), may hold values from -6 to 6
- delay_peak: int32 [128, 128], P('tm', 'chan'), may hold values from 0 to 32767
- rate_peak: int32 [128, 128], P('tm', 'chan'), may hold values from 0 to 15
- station_order: int32 [128], replicated, may hold values from 0 to 127, each once
- ref_station: int32 [1], replicated, may hold values from 0 to 63
Outputs:
- fringe: float32 [128, 128, 2, 8], P('tm', 'chan')
- normal: float32 [128, 2, 256], P('tm', None, 'chan')
- rhs: float32 [128, 2], P('tm')
Inputs may be any that keep to these rules, and one draw needn't show every extreme that they name: `station_order`: each input appears once.
All inputs are finite; a program needn't handle non-finite values.
Results may differ from a plain program's by a relative error of at most 0.0003.
Values sent between devices are 32-bit elements; how exact they have to be, the bound alone decides.
A program may use at most 64 MiB of HBM per device.

v0:
```python
import math
import jax
import jax.numpy as jnp
from jax import lax
from jax.sharding import PartitionSpec as P

BAND = 16384
PERIODS_ALL = 8
WD = 4
WR = 2


def fringe_window(vis_re, vis_im, dpeak, rpeak, chans_total, periods):
    chan_local = vis_re.shape[3]
    dgrid = 2 * BAND
    rgrid = 2 * PERIODS_ALL
    dstep = BAND // chans_total
    rstep = PERIODS_ALL // periods
    chan_idx = jnp.arange(chan_local, dtype=jnp.int32)
    period_idx = jnp.arange(periods, dtype=jnp.int32)
    delays = dpeak[:, :, None] + (jnp.arange(WD, dtype=jnp.int32) - WD // 2) * dstep
    rates = rpeak[:, :, None] + (jnp.arange(WR, dtype=jnp.int32) - WR // 2) * rstep
    dphase = jnp.mod(delays[..., None] * chan_idx, dgrid).astype(jnp.float32) * (
        2.0 * math.pi / dgrid
    )
    rphase = jnp.mod(rates[..., None] * period_idx, rgrid).astype(jnp.float32) * (
        2.0 * math.pi / rgrid
    )
    angle = rphase[:, :, :, None, :, None] + dphase[:, :, None, :, None, :]
    cosine = jnp.cos(angle)
    sine = jnp.sin(angle)
    vr = vis_re[:, :, None, None]
    vi = vis_im[:, :, None, None]
    fre = jnp.sum(vr * cosine + vi * sine, axis=(4, 5))
    fim = jnp.sum(vi * cosine - vr * sine, axis=(4, 5))
    return (fre, fim)


def baseline_weights(fre, fim):
    power = fre * fre + fim * fim
    udel = (2.0 * jnp.arange(WD, dtype=jnp.float32) + 1.0 - WD) / WD
    urat = (2.0 * jnp.arange(WR, dtype=jnp.float32) + 1.0 - WR) / WR
    udel = udel[None, :]
    urat = urat[:, None]
    m_dd = jnp.mean(power * udel * udel, axis=(2, 3))
    m_dr = jnp.mean(power * udel * urat, axis=(2, 3))
    m_rr = jnp.mean(power * urat * urat, axis=(2, 3))
    g_d = jnp.mean(power * udel, axis=(2, 3))
    g_r = jnp.mean(power * urat, axis=(2, 3))
    return jnp.stack([m_dd, m_dr, m_rr, g_d, g_r])


def normal_terms(weights, row_inputs, col_inputs, inputs):
    slots = jnp.arange(inputs, dtype=jnp.int32)
    incidence = (row_inputs[:, None, None] == slots).astype(jnp.float32) - (
        col_inputs[None, :, None] == slots
    ).astype(jnp.float32)
    flat = incidence.reshape(-1, inputs)

    def block(weight):
        scaled = (incidence * weight[:, :, None]).reshape(-1, inputs)
        return jnp.dot(scaled.T, flat, precision=lax.Precision.HIGHEST) / inputs

    n_dd = block(weights[0])
    n_dr = block(weights[1])
    n_rr = block(weights[2])
    normal = jnp.concatenate(
        [jnp.concatenate([n_dd, n_dr], 1), jnp.concatenate([n_dr, n_rr], 1)], 0
    )
    rhs_d = jnp.dot(weights[3].reshape(-1), flat, precision=lax.Precision.HIGHEST) / inputs
    rhs_r = jnp.dot(weights[4].reshape(-1), flat, precision=lax.Precision.HIGHEST) / inputs
    return (normal, jnp.concatenate([rhs_d, rhs_r]))


def full_gram(volts, inputs, scale):
    prod = jnp.einsum("acti,actj->iacj", volts, volts, preferred_element_type=jnp.float32)
    real = prod[:inputs, :, :, :inputs] + prod[inputs:, :, :, inputs:]
    imag = prod[:inputs, :, :, inputs:] - prod[inputs:, :, :, :inputs]
    return jnp.stack([real, imag], axis=3) * scale


def body(volts, delay_peak, rate_peak, station_order, ref_station):
    periods, chans, samples, width = volts.shape
    inputs = width // 2
    row_count = delay_peak.shape[0]
    col_count = delay_peak.shape[1]
    time_devs = lax.axis_size("tm")
    chan_devs = lax.axis_size("chan")
    chans_total = chans * chan_devs
    scale = float(samples * time_devs) ** (-0.5)
    spread = float(periods * chans_total) ** (-0.5)
    col_inputs = lax.dynamic_slice_in_dim(
        station_order, lax.axis_index("chan") * col_count, col_count
    )
    row_inputs = lax.axis_index("tm") * row_count + jnp.arange(row_count, dtype=jnp.int32)
    gram = full_gram(volts, inputs, scale)
    summed = lax.psum_scatter(
        gram.reshape(lax.axis_size("tm") * row_count, -1), "tm", scatter_dimension=0, tiled=True
    )
    vis = summed.reshape(row_count, periods, chans, 2, inputs)
    grouped = jnp.take(vis, station_order, axis=4)
    moved = lax.all_to_all(grouped, "chan", split_axis=4, concat_axis=2, tiled=True)
    vis_re = jnp.transpose(moved[:, :, :, 0], (0, 3, 1, 2))
    vis_im = jnp.transpose(moved[:, :, :, 1], (0, 3, 1, 2))
    fre, fim = fringe_window(vis_re, vis_im, delay_peak, rate_peak, chans_total, periods)
    auto = (row_inputs[:, None] == col_inputs[None, :])[:, :, None, None]
    fre = jnp.where(auto, 0.0, fre * spread)
    fim = jnp.where(auto, 0.0, fim * spread)
    fringe = jnp.stack([fre, fim], axis=2).reshape(row_count, col_count, 2, WR * WD)
    weights = baseline_weights(fre, fim)
    col_width = 2 * inputs // chan_devs
    normal_part, rhs_part = normal_terms(weights, row_inputs, col_inputs, inputs)
    arranged = jnp.transpose(normal_part.reshape(2, inputs, 2 * inputs), (1, 0, 2))
    arranged = arranged.reshape(time_devs, row_count, 2, chan_devs, col_width)
    arranged = jnp.transpose(arranged, (0, 3, 1, 2, 4)).reshape(
        time_devs * chan_devs * row_count, 2, col_width
    )
    normal_rows = lax.psum_scatter(arranged, ("tm", "chan"), scatter_dimension=0, tiled=True)
    rhs_all = lax.psum(jnp.transpose(rhs_part.reshape(2, inputs), (1, 0)), ("tm", "chan"))
    rhs_rows = lax.dynamic_slice_in_dim(rhs_all, lax.axis_index("tm") * row_count, row_count, 0)
    columns = lax.axis_index("chan") * col_width + jnp.arange(col_width, dtype=jnp.int32)
    params = jnp.arange(2, dtype=jnp.int32)[None, :] * inputs + row_inputs[:, None]
    row_ref = row_inputs // 2 == ref_station[0]
    col_ref = columns % inputs // 2 == ref_station[0]
    ident = (params[:, :, None] == columns[None, None, :]).astype(jnp.float32)
    normal_rows = jnp.where(row_ref[:, None, None] | col_ref[None, None, :], ident, normal_rows)
    rhs_rows = jnp.where(row_ref[:, None], 0.0, rhs_rows)
    return (fringe, normal_rows, rhs_rows)


def solution(mesh):
    in_specs = (P(None, "chan", "tm", None), P("tm", "chan"), P("tm", "chan"), P(), P())
    out_specs = (P("tm", "chan", None, None), P("tm", None, "chan"), P("tm", None))
    return jax.shard_map(body, mesh=mesh, in_specs=in_specs, out_specs=out_specs, check_vma=False)
```

profile of v0, /device:TPU:0, one launch (start us, length us, event | category | flops | bytes accessed | tf_op | source)
XLA Modules:
  0.0 298.8 jit_solution(5013165204191400454)
XLA Ops:
  7.2 11.0 %convolution_bitcast_fusion = f32[256,4,4,256]{0,3,2,1:T(8,128)S(1)} fusion(bf16[4,4,1536,256]{3,2,1,0:T(8,128)(2,1)} %param.5), kind=kOutput, calls=%fused_computation.11 | convolution fusion | flops 3221225472 | bytes 16777216 | tf_op jit(solution)/shard_map/acti,actj->iacj/dot_general | solution.py:76
  18.2 0.2 fusion.19
  18.5 0.3 maximum_multiply_fusion
  19.0 1.9 copy.56
  22.3 42.6 %reduce-scatter.7.cloned.1.call-done = f32[16,4096]{1,0:T(8,128)} async-done(((f32[128,4096]{1,0:T(8,128)}), f32[16,4096]{1,0:T(8,128)}) %reduce-scatter.7.cloned.1.call-update) | async-done | bytes 262160
  64.9 1.5 copy.57
  66.5 2.7 copy.41
  69.2 4.9 %gather_fusion = f32[128,16,4,4,2]{1,3,4,2,0:T(4,128)} fusion(f32[16,4,4,2,128]{0,2,4,3,1:T(4,128)} %copy.41, s32[1024]{0:T(1024)S(1)} %pad_clamp_fusion), kind=kCustom, calls=%fused_computation | custom fusion | bytes 524800 | tf_op jit(solution)/shard_map/jit(_take)/gather | solution.py:101
  74.1 2.1 fusion.47
  76.2 2.3 reshape.374
  78.5 4.6 %all-to-all-start = ((f32[4,1,16384]{2,1,0:T(1,128)}), f32[4,1,16384]{2,1,0:T(1,128)S(1)}, u32[]{:S(2)}, u32[]{:S(2)}) async-start(f32[4,1,16384]{2,1,0:T(1,128)} %reshape.374), calls=%async_computation | async-start | bytes 524288 | tf_op jit(solution)/shard_map/all_to_all | solution.py:102
  83.1 1.0 fusion.22
  84.2 7.9 %all-to-all-done = f32[4,1,16384]{2,1,0:T(1,128)S(1)} async-done(((f32[4,1,16384]{2,1,0:T(1,128)}), f32[4,1,16384]{2,1,0:T(1,128)S(1)}, u32[]{:S(2)}, u32[]{:S(2)}) %all-to-all-start) | async-done | bytes 262176 | tf_op jit(solution)/shard_map/all_to_all | solution.py:102
  92.0 0.5 broadcast.559
  92.5 1.4 reduce
  93.9 1.5 reshape.375
  95.4 1.0 copy.42
  96.9 0.6 copy-done
  97.4 16.5 %fusion.5 = (f32[16,32,2,4]{1,3,2,0:T(4,128)S(1)}, f32[16,32,2,4]{1,3,2,0:T(4,128)S(1)}) fusion(f32[16,32,4,16]{1,3,2,0:T(8,128)S(1)} %copy.44, f32[16,32,4,16]{1,3,2,0:T(8,128)S(1)} %copy-done, f32[16,32,2,4]{1,3,2,0:T(4,128)S(1)} %fusion.41, f32[16,32,4,16]{1,3,2,0:T(8,128)S(1)} %copy.43), kind=kLoop, calls=%fused_computation.8 | loop fusion | flops 2351104 | bytes 442368 | tf_op jit(solution)/shard_map/reduce_sum | solution.py:34
  114.2 0.3 fusion.12
  114.5 0.3 fusion.11
  114.8 37.9 %psum.7 = f32[128,2]{0,1:T(2,128)S(1)} all-reduce(f32[128,2]{0,1:T(2,128)S(1)} %maximum_bitcast_fusion), channel_id=1, replica_groups=mesh['tm'=8,'chan'=4] {'tm','chan'}, use_global_device_ids=true, to_apply=%region_9.10 | all-reduce | flops 256 | bytes 2048 | tf_op jit(solution)/shard_map/psum | solution.py:119
  152.7 0.7 fusion.9
  153.4 0.7 fusion.8
  154.1 0.7 fusion.10
  154.9 0.2 reshape.353
  155.2 0.8 copy.48
  156.0 0.7 pad_maximum_fusion
  156.7 0.6 dynamic-slice_select_fusion
  157.3 133.2 %reduce-scatter.5.cloned.1.call-done = f32[16,2,64]{2,0,1:T(8,128)} async-done(((f32[512,2,64]{2,0,1:T(8,128)}), f32[16,2,64]{2,0,1:T(8,128)}) %reduce-scatter.5.cloned.1.call-update) | async-done | bytes 8208 | tf_op jit(solution)/shard_map/reduce_scatter | solution.py:118
  290.6 0.8 convert_select_fusion
  291.4 0.6 copy.49
  (45 shorter events, 2.0 us)
Async XLA Ops:
  7.2 57.8 %reduce-scatter.7.cloned.1.call-start = ((), (), s32[]{:S(2)}) async-start(), calls=%async_computation.4 | async-start | bytes 2359296
  19.0 2.6 copy-start.3
  19.0 3.1 %copy-start.1 = (s32[16,32]{1,0:T(8,128)S(1)}, s32[16,32]{1,0:T(8,128)}, u32[]{:S(2)}) copy-start(s32[16,32]{1,0:T(8,128)} %param.7) | copy-start | bytes 6148
  19.0 3.2 %copy-start.2 = (s32[16,32]{1,0:T(8,128)S(1)}, s32[16,32]{1,0:T(8,128)}, u32[]{:S(2)}) copy-start(s32[16,32]{1,0:T(8,128)} %param.6) | copy-start | bytes 6148
  78.5 13.5 %all-to-all-start = ((f32[4,1,16384]{2,1,0:T(1,128)}), f32[4,1,16384]{2,1,0:T(1,128)S(1)}, u32[]{:S(2)}, u32[]{:S(2)}) async-start(f32[4,1,16384]{2,1,0:T(1,128)} %reshape.374), calls=%async_computation | async-start | bytes 524288 | tf_op jit(solution)/shard_map/all_to_all | solution.py:102
  83.1 207.5 %reduce-scatter.5.cloned.1.call-start = ((), (), s32[]{:S(2)}) async-start(), calls=%async_computation.3 | async-start | bytes 540672 | tf_op jit(solution)/shard_map/reduce_scatter | solution.py:118
  96.4 1.0 copy-start
Sparse Core Ops, SparseCore 0:
  21.0 43.8 reduce-scatter.6
  156.1 134.3 reduce-scatter.4
where the time goes:
time: 299 us
  waiting for transfers between devices  184 us (62%)
  blocking collectives  37.9 us (13%)
  other arithmetic  24.6 us (8%)
  local copies, waits for them, and re-layouts  19.4 us (6%)
  between operations  15 us (5%)
  matrix products  13.6 us (5%)
  starting transfers between devices  4.65 us (2%)
    reduce_scatter x1, waiting for transfers between devices, body(): lax.psum_scatter(arranged, ('tm', 'chan'), scatter_dimension=0, tiled=True)  133 us
    unnamed x3, waiting for transfers between devices  42.6 us
    psum x1, blocking collectives, body(): lax.psum(jnp.transpose(rhs_part.reshape(2, inputs), (1, 0)), ('tm', 'chan'))  37.9 us
    reduce_sum x1, other arithmetic, fringe_window(): fre = jnp.sum(vr * cosine + vi * sine, axis=(4, 5))  16.5 us
    dot_general x1, matrix products, full_gram(): jnp.einsum('acti,actj->iacj', volts, volts, preferred_element_type=jnp.fl...  11 us
    unnamed x13, local copies, waits for them, and re-layouts  8.36 us
    all_to_all x1, waiting for transfers between devices, body(): lax.all_to_all(grouped, 'chan', split_axis=4, concat_axis=2, tiled=True)  7.86 us
  transfers between devices with their start and end apart: 3, of which 3 were waited for; matrix products, arithmetic and copies ran while one was open for 1% of the time, Pallas kernels for 0%

commit v1 on v0

--- a/solution.py
+++ b/solution.py
@@ -8,6 +8,20 @@
 PERIODS_ALL = 8
 WD = 4
 WR = 2
+
+
+def fix_the_axis_part(point, join_dim, state):
+    local_next = point.shape
+    q_next = point.reshape(
+        *local_next[:join_dim], state, local_next[join_dim] // state, *local_next[join_dim + 1 :]
+    )
+    return jnp.moveaxis(q_next, join_dim, 0)
+
+
+def number_tasks(t0, dim_k):
+    state_now = list(t0.shape[1:])
+    state_now[dim_k] *= t0.shape[0]
+    return jnp.moveaxis(t0, 0, dim_k).reshape(state_now)
 
 
 def fringe_window(vis_re, vis_im, dpeak, rpeak, chans_total, periods):
@@ -99,7 +113,18 @@
     )
     vis = summed.reshape(row_count, periods, chans, 2, inputs)
     grouped = jnp.take(vis, station_order, axis=4)
-    moved = lax.all_to_all(grouped, "chan", split_axis=4, concat_axis=2, tiled=True)
+    carry = lax.axis_size("chan")
+    arr_next, w_next = (carry, lax.axis_index("chan"))
+    current_block = fix_the_axis_part(grouped, 4, arr_next)
+    buffer = [current_block[w_next]]
+    for j0 in tuple(range(1, arr_next)):
+        current_value = current_block[w_next ^ j0]
+        buffer.append(
+            lax.ppermute(current_value, "chan", perm=[(pp, pp ^ j0) for pp in range(arr_next)])
+        )
+    part_now = jnp.stack(buffer)
+    current_block = part_now[w_next ^ jnp.arange(arr_next)]
+    moved = number_tasks(current_block, 2)
     vis_re = jnp.transpose(moved[:, :, :, 0], (0, 3, 1, 2))
     vis_im = jnp.transpose(moved[:, :, :, 1], (0, 3, 1, 2))
     fre, fim = fringe_window(vis_re, vis_im, delay_peak, rate_peak, chans_total, periods)

time: 299 us -> 305 us (1.020)
  waiting for transfers between devices: 184 us -> 193 us
  blocking collectives: 37.9 us -> 43.1 us
  local copies, waits for them, and re-layouts: 19.4 us -> 14.9 us
  other arithmetic: 24.6 us -> 21 us
    ppermute x0 -> x3, waiting for transfers between devices: none -> 17.3 us  [body(): lax.ppermute(current_value, 'chan', perm=[(pp, pp ^ j0) for pp in range(a...]
    all_to_all x1 -> x0, waiting for transfers between devices: 7.86 us -> none  [body(): lax.all_to_all(grouped, 'chan', split_axis=4, concat_axis=2, tiled=True)]
    psum x1, blocking collectives: 37.9 us -> 43.1 us  [body(): lax.psum(jnp.transpose(rhs_part.reshape(2, inputs), (1, 0)), ('tm', 'chan'))]
    all_to_all x1 -> x0, starting transfers between devices: 4.61 us -> none  [body(): lax.all_to_all(grouped, 'chan', split_axis=4, concat_axis=2, tiled=True)]
    unnamed x13 -> x9, local copies, waits for them, and re-layouts: 8.36 us -> 4.03 us
    ppermute x0 -> x3, starting transfers between devices: none -> 4.06 us  [body(): lax.ppermute(current_value, 'chan', perm=[(pp, pp ^ j0) for pp in range(a...]
  transfers between devices with their start and end apart: 3 -> 5, of which waited for: 3 -> 4; matrix products, arithmetic and copies ran while one was open for 1% -> 1% of each run, Pallas kernels for 0% -> 0%
where the time goes in v1:
time: 305 us
  waiting for transfers between devices  193 us (63%)
  blocking collectives  43.1 us (14%)
  other arithmetic  21 us (7%)
  between operations  15.1 us (5%)
  local copies, waits for them, and re-layouts  14.9 us (5%)
  matrix products  13.6 us (4%)
  starting transfers between devices  4.33 us (1%)
    reduce_scatter x1, waiting for transfers between devices, body(): lax.psum_scatter(arranged, ('tm', 'chan'), scatter_dimension=0, tiled=True)  134 us
    psum x1, blocking collectives, body(): lax.psum(jnp.transpose(rhs_part.reshape(2, inputs), (1, 0)), ('tm', 'chan'))  43.1 us
    unnamed x3, waiting for transfers between devices  42 us
    ppermute x3, waiting for transfers between devices, body(): lax.ppermute(current_value, 'chan', perm=[(pp, pp ^ j0) for pp in range(a...  17.3 us
    reduce_sum x1, other arithmetic, fringe_window(): fre = jnp.sum(vr * cosine + vi * sine, axis=(4, 5))  16.5 us
    dot_general x1, matrix products, full_gram(): jnp.einsum('acti,actj->iacj', volts, volts, preferred_element_type=jnp.fl...  11 us
  transfers between devices with their start and end apart: 5, of which 4 were waited for; matrix products, arithmetic and copies ran while one was open for 1% of the time, Pallas kernels for 0%

profile of v1, /device:TPU:0, one launch (start us, length us, event | category | flops | bytes accessed | tf_op | source)
XLA Modules:
  0.0 304.8 jit_solution(11636522455981821205)
XLA Ops:
  7.2 11.0 %convolution_bitcast_fusion = f32[256,4,4,256]{0,3,2,1:T(8,128)S(1)} fusion(bf16[4,4,1536,256]{3,2,1,0:T(8,128)(2,1)} %param.5), kind=kOutput, calls=%fused_computation.12 | convolution fusion | flops 3221225472 | bytes 16777216 | tf_op jit(solution)/shard_map/acti,actj->iacj/dot_general | solution.py:90
  18.2 0.2 fusion.19
  18.5 0.3 maximum_multiply_fusion
  19.0 1.9 copy.67
  23.0 41.9 %reduce-scatter.7.cloned.1.call-done = f32[16,4096]{1,0:T(8,128)} async-done(((f32[128,4096]{1,0:T(8,128)}), f32[16,4096]{1,0:T(8,128)}) %reduce-scatter.7.cloned.1.call-update) | async-done | bytes 262160
  64.9 1.5 copy.68
  66.5 2.7 copy.48
  69.2 3.8 %gather_fusion = f32[128,16,4,4,2]{1,3,4,2,0:T(4,128)S(1)} fusion(f32[16,4,4,2,128]{0,2,4,3,1:T(4,128)} %copy.48, s32[1024]{0:T(1024)S(1)} %pad_clamp_fusion.1), kind=kCustom, calls=%fused_computation | custom fusion | bytes 524800 | tf_op jit(solution)/shard_map/jit(_take)/gather | solution.py:115
  73.0 0.5 broadcast_select_fusion
  73.5 0.4 constant_dynamic-slice_fusion.4
  73.9 0.3 copy.51
  74.2 2.5 collective-permute-start.1
  76.7 0.3 copy.52
  77.0 1.5 collective-permute-start.2
  78.5 0.3 copy.50
  79.0 0.3 copy.49
  79.3 16.3 %collective-permute-done.1 = f32[16,4,4,2,32]{4,0,3,2,1:T(8,128)S(1)} collective-permute-done((f32[16,4,4,2,32]{4,0,3,2,1:T(8,128)S(1)}, f32[16,4,4,2,32]{4,0,3,2,1:T(8,128)S(1)}, u32[]{:S(2)}, u32[]{:S(2)}) %collective-permute-start.1) | collective-permute-done | bytes 65568 | tf_op jit(solution)/shard_map/ppermute | solution.py:123
  95.6 1.0 collective-permute-done
  96.7 0.6 gather_fusion.1
  97.9 16.5 %fusion.5 = (f32[16,32,2,4]{1,3,2,0:T(4,128)S(1)}, f32[16,32,2,4]{1,3,2,0:T(4,128)S(1)}) fusion(f32[16,32,4,16]{1,3,2,0:T(8,128)S(1)} %copy.55, f32[16,32,4,16]{1,3,2,0:T(8,128)S(1)} %fusion.22, f32[16,32,2,4]{1,3,2,0:T(4,128)S(1)} %fusion.41, f32[16,32,4,16]{1,3,2,0:T(8,128)S(1)} %copy.54), kind=kLoop, calls=%fused_computation.9 | loop fusion | flops 2351104 | bytes 442368 | tf_op jit(solution)/shard_map/reduce_sum | solution.py:48
  114.7 0.3 fusion.12
  114.9 0.3 fusion.11
  115.3 43.1 %psum.7 = f32[128,2]{0,1:T(2,128)S(1)} all-reduce(f32[128,2]{0,1:T(2,128)S(1)} %maximum_bitcast_fusion), channel_id=1, replica_groups=mesh['tm'=8,'chan'=4] {'tm','chan'}, use_global_device_ids=true, to_apply=%region_9.10 | all-reduce | flops 256 | bytes 2048 | tf_op jit(solution)/shard_map/psum | solution.py:144
  158.4 0.7 fusion.9
  159.1 0.7 fusion.8
  159.8 0.7 fusion.10
  160.9 0.8 copy.59
  161.7 0.7 pad_maximum_fusion.1
  162.4 0.6 fusion.44
  163.0 133.5 %reduce-scatter.5.cloned.1.call-done = f32[16,2,64]{2,0,1:T(8,128)} async-done(((f32[512,2,64]{2,0,1:T(8,128)}), f32[16,2,64]{2,0,1:T(8,128)}) %reduce-scatter.5.cloned.1.call-update) | async-done | bytes 8208 | tf_op jit(solution)/shard_map/reduce_scatter | solution.py:143
  296.6 0.8 convert_select_fusion
  297.4 0.6 copy.60
  (53 shorter events, 3.1 us)
Async XLA Ops:
  7.2 57.8 %reduce-scatter.7.cloned.1.call-start = ((), (), s32[]{:S(2)}) async-start(), calls=%async_computation.3 | async-start | bytes 2359296
  19.0 2.2 copy-start.2
  19.0 3.5 %copy-start = (s32[16,32]{1,0:T(8,128)S(1)}, s32[16,32]{1,0:T(8,128)}, u32[]{:S(2)}) copy-start(s32[16,32]{1,0:T(8,128)} %param.7) | copy-start | bytes 6148
  19.0 3.6 %copy-start.1 = (s32[16,32]{1,0:T(8,128)S(1)}, s32[16,32]{1,0:T(8,128)}, u32[]{:S(2)}) copy-start(s32[16,32]{1,0:T(8,128)} %param.6) | copy-start | bytes 6148
  20.9 275.7 %reduce-scatter.5.cloned.1.call-start = ((), (), s32[]{:S(2)}) async-start(), calls=%async_computation.2 | async-start | bytes 540672 | tf_op jit(solution)/shard_map/reduce_scatter | solution.py:143
  74.2 21.3 %collective-permute-start.1 = (f32[16,4,4,2,32]{4,0,3,2,1:T(8,128)S(1)}, f32[16,4,4,2,32]{4,0,3,2,1:T(8,128)S(1)}, u32[]{:S(2)}, u32[]{:S(2)}) collective-permute-start(f32[16,4,4,2,32]{4,0,3,2,1:T(8,128)S(1)} %bitcast.93), channel_id=1, source_target_pairs={{0,2},{1,3},{2,0},{3,1},{4,6},{5,7},{6,4},{7,5},{8,10},{9,11},{10,... | collective-permute-start | bytes 196616 | tf_op jit(solution)/shard_map/ppermute | solution.py:123
  77.0 18.5 %collective-permute-start.2 = (f32[16,4,4,2,32]{4,0,3,2,1:T(8,128)S(1)}, f32[16,4,4,2,32]{4,0,3,2,1:T(8,128)S(1)}, u32[]{:S(2)}, u32[]{:S(2)}) collective-permute-start(f32[16,4,4,2,32]{4,0,3,2,1:T(8,128)S(1)} %bitcast.94), channel_id=1, source_target_pairs={{0,3},{1,2},{2,1},{3,0},{4,7},{5,6},{6,5},{7,4},{8,11},{9,10},{10,... | collective-permute-start | bytes 196616 | tf_op jit(solution)/shard_map/ppermute | solution.py:123
  78.8 17.7 %collective-permute-start = (f32[16,4,4,2,32]{4,0,3,2,1:T(8,128)S(1)}, f32[16,4,4,2,32]{4,0,3,2,1:T(8,128)S(1)}, u32[]{:S(2)}, u32[]{:S(2)}) collective-permute-start(f32[16,4,4,2,32]{4,0,3,2,1:T(8,128)S(1)} %bitcast.95), channel_id=1, source_target_pairs={{0,1},{1,0},{2,3},{3,2},{4,5},{5,4},{6,7},{7,6},{8,9},{9,8},{10,11... | collective-permute-start | bytes 196616 | tf_op jit(solution)/shard_map/ppermute | solution.py:123
Sparse Core Ops, SparseCore 0:
  21.0 43.8 reduce-scatter.6
  161.8 134.6 reduce-scatter.4
